TPU v7x, 32 devices: a whole 2x2x4 slice. The times are simulated.
32 devices in a mesh: geom: 2 (over x), aux: 16 (over z, y, core).
Axes of the slice: x: 2, y: 2, z: 4, core: 2. Of those that a mesh axis runs over, the one named last changes fastest.
Arguments:
- trial_vecs: float32 [8, 128, 224], P('geom', 'aux'), parts along dimension 0, may hold values from -6 to 6
- occ_energy: float32 [256], P('geom'), parts along dimension 0, may hold values from -1.5 to -0.2
- vir_energy: float32 [448], P('geom'), parts along dimension 0, may hold values from 0.2 to 2.5
- coul_ov: bfloat16 [2048, 128, 224], P(('geom', 'aux')), parts along dimension 0, may hold values from -0.03125 to 0.03125
- exch_oo: bfloat16 [2048, 128, 128], P(('geom', 'aux')), parts along dimension 0, may hold values from -0.0234375 to 0.0234375
- exch_vv: bfloat16 [2048, 224, 224], P(('geom', 'aux')), parts along dimension 0, may hold values from -0.375 to 0.375
Outputs:
- sigma_vecs: float32 [8, 128, 224], P('geom', 'aux'), parts along dimension 0
- update_vecs: float32 [8, 128, 224], P('geom', 'aux'), parts along dimension 0
There are 2 independent parts, one for each index of `geom`. A program takes and returns all parts, laid end to end along the dimension named above; each array names one. Nothing has to cross between parts.
All inputs are finite; a program needn't handle non-finite values.
Results may differ from a plain program's by a relative error of at most 0.0037.
Values may be sent and summed in bfloat16 or wider, within the bound.
No kernel may reach another device: no remote copies, remote signals or barrier semaphores. Data moves between devices by JAX's collectives and lax.ppermute only.
A program may use at most 64 MiB of HBM per device.

v0:
```python
import math
import jax
import jax.numpy as jnp
from jax import lax
from jax.sharding import PartitionSpec as P


def contract(totals, rows_x, coul_ov, exch_oo, exch_vv):
    aux_coef, exchange = totals
    height = rows_x.shape[1]
    n_occ = exch_oo.shape[1]
    n_virt = exch_vv.shape[1]
    aux_coef = jnp.einsum("pia,nia->np", coul_ov, rows_x, preferred_element_type=jnp.float32)
    aux_local = exch_vv.shape[0]
    group_size = math.gcd(aux_local, 16)
    group_count = aux_local // group_size
    vv_groups = exch_vv.reshape(group_count, group_size, n_virt, n_virt)
    oo_groups = exch_oo.reshape(group_count, group_size, n_occ, height)

    def advance(running, parts_pair):
        vv_part, oo_part = parts_pair
        halfway = jnp.einsum(
            "pab,njb->pnja", vv_part, rows_x, preferred_element_type=jnp.float32
        ).astype(jnp.bfloat16)
        return (
            running
            + jnp.einsum("pij,pnja->nia", oo_part, halfway, preferred_element_type=jnp.float32),
            None,
        )

    exchange, _ = lax.scan(advance, exchange, (vv_groups, oo_groups))
    return (aux_coef, exchange)


def residual_step(sigma_part, trial_part, diagonal, omega):
    resid = sigma_part - omega[:, None, None] * trial_part
    gap = jnp.maximum(jnp.abs(diagonal[None] - omega[:, None, None]), 1.0)
    return resid / gap


def on_device(trial_vecs, occ_energy, vir_energy, coul_ov, exch_oo, exch_vv):
    n_trial = trial_vecs.shape[0]
    local_rows = trial_vecs.shape[1]
    n_virt = trial_vecs.shape[2]
    n_occ = exch_oo.shape[1]
    aux_local = coul_ov.shape[0]
    empty = (
        jnp.zeros((n_trial, aux_local), jnp.float32),
        jnp.zeros((n_trial, n_occ, n_virt), jnp.float32),
    )
    row_start = lax.axis_index("aux") * local_rows
    wide_x = lax.all_gather(trial_vecs, "aux", axis=1, tiled=True)
    aux_coef, exchange = contract(empty, wide_x.astype(jnp.bfloat16), coul_ov, exch_oo, exch_vv)
    coulomb = jnp.einsum(
        "pia,np->nia", coul_ov, aux_coef.astype(jnp.bfloat16), preferred_element_type=jnp.float32
    )
    summed = lax.psum(2.0 * coulomb - exchange, "aux")
    diagonal = vir_energy[None, :] - occ_energy[:, None]
    sigma_all = diagonal[None] * wide_x + summed
    omega = jnp.sum(wide_x * sigma_all, axis=(1, 2)) / (
        jnp.sum(wide_x * wide_x, axis=(1, 2)) + 1e-06
    )
    precond = residual_step(sigma_all, wide_x, diagonal, omega)
    update_all = (
        precond * lax.rsqrt(jnp.mean(precond * precond, axis=(1, 2)) + 1e-06)[:, None, None]
    )
    sigma_vecs = lax.dynamic_slice_in_dim(sigma_all, row_start, local_rows, 1)
    update_vecs = lax.dynamic_slice_in_dim(update_all, row_start, local_rows, 1)
    return (sigma_vecs, update_vecs)


def solution(mesh):
    in_specs = (
        P("geom", "aux", None),
        P("geom"),
        P("geom"),
        P(("geom", "aux"), None, None),
        P(("geom", "aux"), None, None),
        P(("geom", "aux"), None, None),
    )
    out_specs = (P("geom", "aux", None), P("geom", "aux", None))
    return jax.shard_map(
        on_device, mesh=mesh, in_specs=in_specs, out_specs=out_specs, check_vma=False
    )
```

profile of v0, /device:TPU:0, one launch (start us, length us, event | category | flops | bytes accessed | tf_op | source)
XLA Modules:
  0.0 160.3 jit_solution(4688570363606826687)
XLA Ops:
  7.2 0.0 all-reduce.2.cloned.1.call-start
  7.2 0.8 copy.23
  8.0 24.6 %all_gather.3 = f32[4,128,224]{2,0,1:T(4,128)S(1)} all-gather(f32[4,8,224]{2,0,1:T(4,128)S(1)} %copy.23), channel_id=1, replica_groups=mesh['geom'=2,'aux'=16] {'aux'}, dimensions={1}, use_global_device_ids=true | all-gather | bytes 487424 | tf_op jit(solution)/shard_map/all_gather | solution.py:52
  32.6 0.4 multiply_reduce_fusion
  33.0 6.8 %copy.25 = bf16[64,128,224]{2,0,1:T(8,128)(2,1)} copy(bf16[64,128,224]{1,2,0:T(8,128)(2,1)} %param.11) | data formatting | bytes 7340032 | tf_op args[3]
  39.8 0.2 copy.28
  40.0 6.1 %fusion.25 = f32[4,128,224]{1,0,2:T(4,128)S(1)} fusion(bf16[64,128,224]{1,2,0:T(8,128)(2,1)} %param.11, bf16[4,128,224]{2,0,1:T(4,128)(2,1)S(1)} %get-tuple-element.84, bf16[64,128,224]{2,0,1:T(8,128)(2,1)} %copy.25), kind=kOutput, calls=%fused_computation.12 | convolution fusion | flops 29360384 | bytes 8028160 | tf_op jit(solution)/shard_map/pia,np->nia/dot_general | solution.py:54
  46.1 15.2 %while.11 = (s32[]{:T(128)}, f32[4,128,224]{1,2,0:T(8,128)S(1)}, bf16[4,16,224,224]{3,2,1,0:T(8,128)(2,1)}, bf16[4,128,224]{1,2,0:T(8,128)(2,1)S(1)}, bf16[4,16,...) while((s32[]{:T(128)}, f32[4,128,224]{1,2,0:T(8,128)S(1)}, ...), condition=%wide.region_1.2_spmd.clone, body=%wide.region_0.1_spmd.clone.sunk | while | flops 1293910016 | bytes 3507287 | solution.py:31
  46.1 3.8 %fusion.41 = f32[4,128,224]{1,2,0:T(8,128)S(1)} fusion(bf16[4,16,224,224]{3,2,1,0:T(8,128)(2,1)} %get-tuple-element.134, s32[]{:T(128)} %get-tuple-element.125, bf16[4,16,128,128]{3,2,1,0:T(8,128)(2,1)} %get-tuple-element.136, f32[4,128,224]{1,2,0:T(8,128)S(1)} %get-tuple-element.126, bf16[4,128,224]{1,2,0:T(8,128)(2,1)S(1)} %get-tuple-element.135, ...), kind=kOutput, calls=%fused_computation.7.clone.1 | convolution fusion | flops 1293910016 | bytes 3507201 | tf_op jit(solution)/shard_map/while/body/eval_jaxpr/pij,pnja->nia/dot_general | solution.py:27
  49.9 3.8 %fusion.41 = f32[4,128,224]{1,2,0:T(8,128)S(1)} fusion(bf16[4,16,224,224]{3,2,1,0:T(8,128)(2,1)} %get-tuple-element.134, s32[]{:T(128)} %get-tuple-element.125, bf16[4,16,128,128]{3,2,1,0:T(8,128)(2,1)} %get-tuple-element.136, f32[4,128,224]{1,2,0:T(8,128)S(1)} %get-tuple-element.126, bf16[4,128,224]{1,2,0:T(8,128)(2,1)S(1)} %get-tuple-element.135, ...), kind=kOutput, calls=%fused_computation.7.clone.1 | convolution fusion | flops 1293910016 | bytes 3507201 | tf_op jit(solution)/shard_map/while/body/eval_jaxpr/pij,pnja->nia/dot_general | solution.py:27
  53.7 3.8 %fusion.41 = f32[4,128,224]{1,2,0:T(8,128)S(1)} fusion(bf16[4,16,224,224]{3,2,1,0:T(8,128)(2,1)} %get-tuple-element.134, s32[]{:T(128)} %get-tuple-element.125, bf16[4,16,128,128]{3,2,1,0:T(8,128)(2,1)} %get-tuple-element.136, f32[4,128,224]{1,2,0:T(8,128)S(1)} %get-tuple-element.126, bf16[4,128,224]{1,2,0:T(8,128)(2,1)S(1)} %get-tuple-element.135, ...), kind=kOutput, calls=%fused_computation.7.clone.1 | convolution fusion | flops 1293910016 | bytes 3507201 | tf_op jit(solution)/shard_map/while/body/eval_jaxpr/pij,pnja->nia/dot_general | solution.py:27
  57.5 3.8 %fusion.41 = f32[4,128,224]{1,2,0:T(8,128)S(1)} fusion(bf16[4,16,224,224]{3,2,1,0:T(8,128)(2,1)} %get-tuple-element.134, s32[]{:T(128)} %get-tuple-element.125, bf16[4,16,128,128]{3,2,1,0:T(8,128)(2,1)} %get-tuple-element.136, f32[4,128,224]{1,2,0:T(8,128)S(1)} %get-tuple-element.126, bf16[4,128,224]{1,2,0:T(8,128)(2,1)S(1)} %get-tuple-element.135, ...), kind=kOutput, calls=%fused_computation.7.clone.1 | convolution fusion | flops 1293910016 | bytes 3507201 | tf_op jit(solution)/shard_map/while/body/eval_jaxpr/pij,pnja->nia/dot_general | solution.py:27
  61.3 0.8 fusion.29
  62.1 0.0 all-reduce.2.cloned.1.call-update
  62.2 0.2 copy.24
  62.4 0.0 copy-done
  62.4 0.0 copy-done.1
  62.4 0.1 broadcast_subtract_fusion
  62.5 87.5 %all-reduce.2.cloned.1.call-done = f32[4,128,224]{1,2,0:T(8,128)} async-done(((f32[4,128,224]{1,2,0:T(8,128)}), f32[4,128,224]{1,2,0:T(8,128)}) %all-reduce.2.cloned.1.call-update) | async-done | bytes 458768 | tf_op jit(solution)/shard_map/psum | solution.py:57
  150.1 1.2 multiply_reduce_fusion.2
  151.3 0.3 multiply_reduce_fusion.1
  151.6 0.3 dynamic-slice_multiply_fusion
  151.9 0.8 copy.31
  152.7 0.8 copy.32
  (5 shorter events, 0.0 us)
Async XLA Ops:
  7.2 142.9 %all-reduce.2.cloned.1.call-start = ((), (), s32[]{:S(2)}) async-start(), calls=%async_computation | async-start | bytes 917504 | tf_op jit(solution)/shard_map/psum | solution.py:57
  46.1 16.3 %copy-start = (f32[224]{0:T(256)S(1)}, f32[224]{0:T(256)}, u32[]{:S(2)}) copy-start(f32[224]{0:T(256)} %param.10) | copy-start | bytes 2692
  46.1 16.3 %copy-start.1 = (f32[128]{0:T(128)S(1)}, f32[128]{0:T(128)}, u32[]{:S(2)}) copy-start(f32[128]{0:T(128)} %param.9) | copy-start | bytes 1540
Sparse Core Ops, SparseCore 0:
  62.3 87.7 all-reduce.1
where the time goes:
time: 161 us; the launch traced here: 160 us
  waiting for transfers between devices  87.6 us (54%)
  blocking collectives  24.6 us (15%)
  matrix products  21.2 us (13%)
  between operations  14.1 us (9%)
  local copies, waits for them, and re-layouts  9.57 us (6%)
  other arithmetic  3.17 us (2%)
    psum x1, waiting for transfers between devices, on_device(): summed = lax.psum(2.0 * coulomb - exchange, 'aux')  87.5 us
    all_gather x1, blocking collectives, on_device(): wide_x = lax.all_gather(trial_vecs, 'aux', axis=1, tiled=True)  24.6 us
    dot_general x4, matrix products, advance(): jnp.einsum('pij,pnja->nia', oo_part, halfway, preferred_element_type=jnp....  15.1 us
    unnamed x9, local copies, waits for them, and re-layouts  9.34 us
    dot_general x1, matrix products, on_device(): jnp.einsum('pia,np->nia', coul_ov, aux_coef.astype(jnp.bfloat16), preferr...  6.1 us
  transfers between devices with their start and end apart: 1, of which 1 were waited for; matrix products, arithmetic and copies ran while one was open for 0% of the time, Pallas kernels for 0%

commit v1 on v0

--- a/solution.py
+++ b/solution.py
@@ -49,7 +49,19 @@
         jnp.zeros((n_trial, n_occ, n_virt), jnp.float32),
     )
     row_start = lax.axis_index("aux") * local_rows
-    wide_x = lax.all_gather(trial_vecs, "aux", axis=1, tiled=True)
+    n_dev_all = lax.axis_size("aux")
+    shelf = tuple(((b, (b + 1) % n_dev_all) for b in range(n_dev_all)))
+    slots = tuple(((b, (b - 1) % n_dev_all) for b in range(n_dev_all)))
+    v1, e_now = ([trial_vecs], [trial_vecs])
+    for _ in range(n_dev_all // 2):
+        v1.append(lax.ppermute(v1[-1], "aux", shelf))
+    for _ in range((n_dev_all - 1) // 2):
+        e_now.append(lax.ppermute(e_now[-1], "aux", slots))
+    wide_x = jnp.roll(
+        jnp.concatenate([*v1[::-1], *e_now[1:]], axis=1),
+        (lax.axis_index("aux") - n_dev_all // 2) * trial_vecs.shape[1],
+        axis=1,
+    )
     aux_coef, exchange = contract(empty, wide_x.astype(jnp.bfloat16), coul_ov, exch_oo, exch_vv)
     coulomb = jnp.einsum(
         "pia,np->nia", coul_ov, aux_coef.astype(jnp.bfloat16), preferred_element_type=jnp.float32

time: 161 us -> 251 us (1.56)
  starting transfers between devices: 0.04 us -> 55.7 us
  waiting for transfers between devices: 87.6 us -> 132 us
  blocking collectives: 24.6 us -> 0 us
  local copies, waits for them, and re-layouts: 9.57 us -> 20.2 us
  matrix products: 21.2 us -> 25.2 us
    ppermute x0 -> x15, starting transfers between devices: none -> 55.7 us  [the longest x8 46.2 us: on_device(): v1.append(lax.ppermute(v1[-1], 'aux', shelf))]
    ppermute x0 -> x15, waiting for transfers between devices: none -> 35.6 us  [the longest x8 35.6 us: on_device(): v1.append(lax.ppermute(v1[-1], 'aux', shelf))]
    all_gather x1 -> x0, blocking collectives: 24.6 us -> none  [on_device(): wide_x = lax.all_gather(trial_vecs, 'aux', axis=1, tiled=True)]
    concatenate x0 -> x1, local copies, waits for them, and re-layouts: none -> 17.2 us  [on_device(): jnp.roll(jnp.concatenate([*v1[::-1], *e_now[1:]], axis=1), (lax.axis_inde...]
    psum x1, waiting for transfers between devices: 87.5 us -> 96.4 us  [on_device(): summed = lax.psum(2.0 * coulomb - exchange, 'aux')]
    unnamed x9 -> x22, local copies, waits for them, and re-layouts: 9.34 us -> 2.77 us
    dot_general x4, matrix products: 15.1 us -> 18.3 us  [advance(): jnp.einsum('pij,pnja->nia', oo_part, halfway, preferred_element_type=jnp....]
  transfers between devices with their start and end apart: 1 -> 16, of which waited for: 1 -> 9; matrix products, arithmetic and copies ran while one was open for 0% -> 0% of each run, Pallas kernels for 0% -> 0%
where the time goes in v1:
time: 251 us; the launch traced here: 250 us
  waiting for transfers between devices  132 us (53%)
  starting transfers between devices  55.7 us (22%)
  matrix products  25.2 us (10%)
  local copies, waits for them, and re-layouts  20.2 us (8%)
  between operations  14.1 us (6%)
  other arithmetic  2.67 us (1%)
    psum x1, waiting for transfers between devices, on_device(): summed = lax.psum(2.0 * coulomb - exchange, 'aux')  96.4 us
    ppermute x8, starting transfers between devices, on_device(): v1.append(lax.ppermute(v1[-1], 'aux', shelf))  46.2 us
    ppermute x8, waiting for transfers between devices, on_device(): v1.append(lax.ppermute(v1[-1], 'aux', shelf))  35.6 us
    dot_general x4, matrix products, advance(): jnp.einsum('pij,pnja->nia', oo_part, halfway, preferred_element_type=jnp....  18.3 us
    concatenate x1, local copies, waits for them, and re-layouts, on_device(): jnp.roll(jnp.concatenate([*v1[::-1], *e_now[1:]], axis=1), (lax.axis_inde...  17.2 us
    ppermute x7, starting transfers between devices, on_device(): e_now.append(lax.ppermute(e_now[-1], 'aux', slots))  9.48 us
    dot_general x1, matrix products, on_device(): jnp.einsum('pia,np->nia', coul_ov, aux_coef.astype(jnp.bfloat16), preferr...  6.88 us
  transfers between devices with their start and end apart: 16, of which 9 were waited for; matrix products, arithmetic and copies ran while one was open for 0% of the time, Pallas kernels for 0%

profile of v1, /device:TPU:0, one launch (start us, length us, event | category | flops | bytes accessed | tf_op | source)
XLA Modules:
  0.0 249.9 jit_solution(9001120703639517823)
XLA Ops:
  8.7 5.0 %collective-permute-start.8 = (f32[4,8,224]{1,0,2:T(4,128)S(1)}, f32[4,8,224]{1,0,2:T(4,128)S(1)}, u32[]{:S(2)}, u32[]{:S(2)}) collective-permute-start(f32[4,8,224]{1,0,2:T(4,128)S(1)} %copy.8), channel_id=1, source_target_pairs={{0,15},{1,0},{2,1},{3,2},{4,3},{5,4},{6,5},{7,6},{8,7},{9,8},{10,9... | collective-permute-start | bytes 86024 | tf_op jit(solution)/shard_map/ppermute | solution.py:59
  13.8 6.2 %collective-permute-done = f32[4,8,224]{1,0,2:T(4,128)S(1)} collective-permute-done((f32[4,8,224]{1,0,2:T(4,128)S(1)}, f32[4,8,224]{1,0,2:T(4,128)S(1)}, u32[]{:S(2)}, u32[]{:S(2)}) %collective-permute-start) | collective-permute-done | bytes 28704 | tf_op jit(solution)/shard_map/ppermute | solution.py:57
  21.7 2.8 %collective-permute-start.9 = (f32[4,8,224]{1,0,2:T(4,128)S(1)}, f32[4,8,224]{1,0,2:T(4,128)S(1)}, u32[]{:S(2)}, u32[]{:S(2)}) collective-permute-start(f32[4,8,224]{1,0,2:T(4,128)S(1)} %collective-permute-done.8), channel_id=1, source_target_pairs={{0,15},{1,0},{2,1},{3,2},{4,3},{5,4},{6,5},{7,6},{8,7},{9,8},{10,9... | collective-permute-start | bytes 86024 | tf_op jit(solution)/shard_map/ppermute | solution.py:59
  24.5 6.2 %collective-permute-done.1 = f32[4,8,224]{1,0,2:T(4,128)S(1)} collective-permute-done((f32[4,8,224]{1,0,2:T(4,128)S(1)}, f32[4,8,224]{1,0,2:T(4,128)S(1)}, u32[]{:S(2)}, u32[]{:S(2)}) %collective-permute-start.1) | collective-permute-done | bytes 28704 | tf_op jit(solution)/shard_map/ppermute | solution.py:57
  30.7 3.1 %collective-permute-start.2 = (f32[4,8,224]{1,0,2:T(4,128)S(1)}, f32[4,8,224]{1,0,2:T(4,128)S(1)}, u32[]{:S(2)}, u32[]{:S(2)}) collective-permute-start(f32[4,8,224]{1,0,2:T(4,128)S(1)} %collective-permute-done.1), channel_id=1, source_target_pairs={{0,1},{1,2},{2,3},{3,4},{4,5},{5,6},{6,7},{7,8},{8,9},{9,10},{10,1... | collective-permute-start | bytes 86024 | tf_op jit(solution)/shard_map/ppermute | solution.py:57
  35.2 6.2 %collective-permute-done.2 = f32[4,8,224]{1,0,2:T(4,128)S(1)} collective-permute-done((f32[4,8,224]{1,0,2:T(4,128)S(1)}, f32[4,8,224]{1,0,2:T(4,128)S(1)}, u32[]{:S(2)}, u32[]{:S(2)}) %collective-permute-start.2) | collective-permute-done | bytes 28704 | tf_op jit(solution)/shard_map/ppermute | solution.py:57
  41.4 4.4 %collective-permute-start.3 = (f32[4,8,224]{1,0,2:T(4,128)S(1)}, f32[4,8,224]{1,0,2:T(4,128)S(1)}, u32[]{:S(2)}, u32[]{:S(2)}) collective-permute-start(f32[4,8,224]{1,0,2:T(4,128)S(1)} %collective-permute-done.2), channel_id=1, source_target_pairs={{0,1},{1,2},{2,3},{3,4},{4,5},{5,6},{6,7},{7,8},{8,9},{9,10},{10,1... | collective-permute-start | bytes 86024 | tf_op jit(solution)/shard_map/ppermute | solution.py:57
  45.9 6.1 %collective-permute-done.3 = f32[4,8,224]{1,0,2:T(4,128)S(1)} collective-permute-done((f32[4,8,224]{1,0,2:T(4,128)S(1)}, f32[4,8,224]{1,0,2:T(4,128)S(1)}, u32[]{:S(2)}, u32[]{:S(2)}) %collective-permute-start.3) | collective-permute-done | bytes 28704 | tf_op jit(solution)/shard_map/ppermute | solution.py:57
  52.0 6.6 %collective-permute-start.4 = (f32[4,8,224]{1,0,2:T(4,128)S(1)}, f32[4,8,224]{1,0,2:T(4,128)S(1)}, u32[]{:S(2)}, u32[]{:S(2)}) collective-permute-start(f32[4,8,224]{1,0,2:T(4,128)S(1)} %collective-permute-done.3), channel_id=1, source_target_pairs={{0,1},{1,2},{2,3},{3,4},{4,5},{5,6},{6,7},{7,8},{8,9},{9,10},{10,1... | collective-permute-start | bytes 86024 | tf_op jit(solution)/shard_map/ppermute | solution.py:57
  58.7 4.0 %collective-permute-done.4 = f32[4,8,224]{1,0,2:T(4,128)S(1)} collective-permute-done((f32[4,8,224]{1,0,2:T(4,128)S(1)}, f32[4,8,224]{1,0,2:T(4,128)S(1)}, u32[]{:S(2)}, u32[]{:S(2)}) %collective-permute-start.4) | collective-permute-done | bytes 28704 | tf_op jit(solution)/shard_map/ppermute | solution.py:57
  62.6 8.8 %collective-permute-start.5 = (f32[4,8,224]{1,0,2:T(4,128)S(1)}, f32[4,8,224]{1,0,2:T(4,128)S(1)}, u32[]{:S(2)}, u32[]{:S(2)}) collective-permute-start(f32[4,8,224]{1,0,2:T(4,128)S(1)} %collective-permute-done.4), channel_id=1, source_target_pairs={{0,1},{1,2},{2,3},{3,4},{4,5},{5,6},{6,7},{7,8},{8,9},{9,10},{10,1... | collective-permute-start | bytes 86024 | tf_op jit(solution)/shard_map/ppermute | solution.py:57
  71.5 2.1 collective-permute-done.5
  73.6 10.6 %collective-permute-start.6 = (f32[4,8,224]{1,0,2:T(4,128)S(1)}, f32[4,8,224]{1,0,2:T(4,128)}, u32[]{:S(2)}, u32[]{:S(2)}) collective-permute-start(f32[4,8,224]{1,0,2:T(4,128)S(1)} %collective-permute-done.5), channel_id=1, source_target_pairs={{0,1},{1,2},{2,3},{3,4},{4,5},{5,6},{6,7},{7,8},{8,9},{9,10},{10,1... | collective-permute-start | bytes 86024 | tf_op jit(solution)/shard_map/ppermute | solution.py:57
  84.3 2.3 collective-permute-done.6
  86.6 10.5 %collective-permute-start.7 = (f32[4,8,224]{1,0,2:T(4,128)}, f32[4,8,224]{1,0,2:T(4,128)}, u32[]{:S(2)}, u32[]{:S(2)}) collective-permute-start(f32[4,8,224]{1,0,2:T(4,128)} %collective-permute-done.6), channel_id=1, source_target_pairs={{0,1},{1,2},{2,3},{3,4},{4,5},{5,6},{6,7},{7,8},{8,9},{9,10},{10,1... | collective-permute-start | bytes 86024 | tf_op jit(solution)/shard_map/ppermute | solution.py:57
  97.1 2.5 collective-permute-done.7
  99.5 17.2 %concatenate.6 = f32[4,256,224]{1,0,2:T(4,128)S(1)} concatenate(f32[4,8,224]{1,0,2:T(4,128)} %collective-permute-done.7, f32[4,8,224]{1,0,2:T(4,128)} %collective-permute-done.6, f32[4,8,224]{1,0,2:T(4,128)} %copy-done.6, f32[4,8,224]{1,0,2:T(4,128)} %copy-done.4, f32[4,8,224]{1,0,2:T(4,128)} %copy-done.2, f32[4,8,224]{1,0,2:T(4,128)} %copy-done, ...), dimensions={1} | concatenate | bytes 1835008 | tf_op jit(solution)/shard_map/jit(_roll_dynamic)/concatenate | solution.py:60
  117.2 18.3 %while.11 = (s32[]{:T(128)}, f32[4,128,224]{1,2,0:T(8,128)}, bf16[4,16,224,224]{3,2,1,0:T(8,128)(2,1)}, bf16[4,128,224]{2,1,0:T(8,128)(2,1)S(1)}, bf16[4,16,128,128]{3,2,1,0:T(8,128)(2,1)}, /*index=5*/s32[]{:T(128)}, s32[]{:T(128)}) while((s32[]{:T(128)}, f32[4,128,224]{1,2,0:T(8,128)}, bf16[4,16,224,224]{3,2,1,0:T(8,128)(2,1)}, ...), condition=%wide.region_1.2_spmd.clone, body=%wide.region_0.1_spmd.clone.sunk | while | flops 1293910016 | bytes 3507287 | solution.py:31
  117.2 4.5 %fusion.56 = f32[4,128,224]{1,2,0:T(8,128)} fusion(bf16[4,16,224,224]{3,2,1,0:T(8,128)(2,1)} %get-tuple-element.119, s32[]{:T(128)} %get-tuple-element.110, bf16[4,16,128,128]{3,2,1,0:T(8,128)(2,1)} %get-tuple-element.121, f32[4,128,224]{1,2,0:T(8,128)} %get-tuple-element.111, bf16[4,128,224]{2,1,0:T(8,128)(2,1)S(1)} %get-tuple-element.120, ...), kind=kOutput, calls=%fused_computation.7.clone.1 | convolution fusion | flops 1293910016 | bytes 3507201 | tf_op jit(solution)/shard_map/while/body/eval_jaxpr/pij,pnja->nia/dot_general | solution.py:27
  121.6 4.6 %fusion.56 = f32[4,128,224]{1,2,0:T(8,128)} fusion(bf16[4,16,224,224]{3,2,1,0:T(8,128)(2,1)} %get-tuple-element.119, s32[]{:T(128)} %get-tuple-element.110, bf16[4,16,128,128]{3,2,1,0:T(8,128)(2,1)} %get-tuple-element.121, f32[4,128,224]{1,2,0:T(8,128)} %get-tuple-element.111, bf16[4,128,224]{2,1,0:T(8,128)(2,1)S(1)} %get-tuple-element.120, ...), kind=kOutput, calls=%fused_computation.7.clone.1 | convolution fusion | flops 1293910016 | bytes 3507201 | tf_op jit(solution)/shard_map/while/body/eval_jaxpr/pij,pnja->nia/dot_general | solution.py:27
  126.3 4.6 %fusion.56 = f32[4,128,224]{1,2,0:T(8,128)} fusion(bf16[4,16,224,224]{3,2,1,0:T(8,128)(2,1)} %get-tuple-element.119, s32[]{:T(128)} %get-tuple-element.110, bf16[4,16,128,128]{3,2,1,0:T(8,128)(2,1)} %get-tuple-element.121, f32[4,128,224]{1,2,0:T(8,128)} %get-tuple-element.111, bf16[4,128,224]{2,1,0:T(8,128)(2,1)S(1)} %get-tuple-element.120, ...), kind=kOutput, calls=%fused_computation.7.clone.1 | convolution fusion | flops 1293910016 | bytes 3507201 | tf_op jit(solution)/shard_map/while/body/eval_jaxpr/pij,pnja->nia/dot_general | solution.py:27
  130.9 4.6 %fusion.56 = f32[4,128,224]{1,2,0:T(8,128)} fusion(bf16[4,16,224,224]{3,2,1,0:T(8,128)(2,1)} %get-tuple-element.119, s32[]{:T(128)} %get-tuple-element.110, bf16[4,16,128,128]{3,2,1,0:T(8,128)(2,1)} %get-tuple-element.121, f32[4,128,224]{1,2,0:T(8,128)} %get-tuple-element.111, bf16[4,128,224]{2,1,0:T(8,128)(2,1)S(1)} %get-tuple-element.120, ...), kind=kOutput, calls=%fused_computation.7.clone.1 | convolution fusion | flops 1293910016 | bytes 3507201 | tf_op jit(solution)/shard_map/while/body/eval_jaxpr/pij,pnja->nia/dot_general | solution.py:27
  135.5 6.9 %fusion.32 = f32[4,128,224]{1,0,2:T(4,128)} fusion(bf16[64,128,224]{1,2,0:T(8,128)(2,1)} %param.11, bf16[4,128,224]{1,0,2:T(4,128)(2,1)S(1)} %dynamic-slice_convert_fusion, f32[4,128,224]{1,2,0:T(8,128)} %get-tuple-element.29), kind=kOutput, calls=%fused_computation.17 | convolution fusion | flops 29589760 | bytes 4816896 | tf_op jit(solution)/shard_map/pia,np->nia/dot_general | solution.py:66
  142.5 96.4 %all-reduce.2.cloned.1.call-done = f32[4,128,224]{1,0,2:T(4,128)} async-done(((f32[4,128,224]{1,0,2:T(4,128)}), f32[4,128,224]{1,0,2:T(4,128)}) %all-reduce.2.cloned.1.call-update) | async-done | bytes 458768 | tf_op jit(solution)/shard_map/psum | solution.py:69
  (46 shorter events, 9.6 us)
Async XLA Ops:
  7.2 231.7 %all-reduce.2.cloned.1.call-start = ((), (), s32[]{:S(2)}) async-start(), calls=%async_computation | async-start | bytes 917504 | tf_op jit(solution)/shard_map/psum | solution.py:69
  8.2 11.8 %collective-permute-start = (f32[4,8,224]{1,0,2:T(4,128)S(1)}, f32[4,8,224]{1,0,2:T(4,128)S(1)}, u32[]{:S(2)}, u32[]{:S(2)}) collective-permute-start(f32[4,8,224]{1,0,2:T(4,128)S(1)} %copy.8), channel_id=1, source_target_pairs={{0,1},{1,2},{2,3},{3,4},{4,5},{5,6},{6,7},{7,8},{8,9},{9,10},{10,1... | collective-permute-start | bytes 86024 | tf_op jit(solution)/shard_map/ppermute | solution.py:57
  8.7 13.0 %collective-permute-start.8 = (f32[4,8,224]{1,0,2:T(4,128)S(1)}, f32[4,8,224]{1,0,2:T(4,128)S(1)}, u32[]{:S(2)}, u32[]{:S(2)}) collective-permute-start(f32[4,8,224]{1,0,2:T(4,128)S(1)} %copy.8), channel_id=1, source_target_pairs={{0,15},{1,0},{2,1},{3,2},{4,3},{5,4},{6,5},{7,6},{8,7},{9,8},{10,9... | collective-permute-start | bytes 86024 | tf_op jit(solution)/shard_map/ppermute | solution.py:59
  20.0 10.7 %collective-permute-start.1 = (f32[4,8,224]{1,0,2:T(4,128)S(1)}, f32[4,8,224]{1,0,2:T(4,128)S(1)}, u32[]{:S(2)}, u32[]{:S(2)}) collective-permute-start(f32[4,8,224]{1,0,2:T(4,128)S(1)} %collective-permute-done), channel_id=1, source_target_pairs={{0,1},{1,2},{2,3},{3,4},{4,5},{5,6},{6,7},{7,8},{8,9},{9,10},{10,1... | collective-permute-start | bytes 86024 | tf_op jit(solution)/shard_map/ppermute | solution.py:57
  21.7 12.0 %collective-permute-start.9 = (f32[4,8,224]{1,0,2:T(4,128)S(1)}, f32[4,8,224]{1,0,2:T(4,128)S(1)}, u32[]{:S(2)}, u32[]{:S(2)}) collective-permute-start(f32[4,8,224]{1,0,2:T(4,128)S(1)} %collective-permute-done.8), channel_id=1, source_target_pairs={{0,15},{1,0},{2,1},{3,2},{4,3},{5,4},{6,5},{7,6},{8,7},{9,8},{10,9... | collective-permute-start | bytes 86024 | tf_op jit(solution)/shard_map/ppermute | solution.py:59
  30.7 10.7 %collective-permute-start.2 = (f32[4,8,224]{1,0,2:T(4,128)S(1)}, f32[4,8,224]{1,0,2:T(4,128)S(1)}, u32[]{:S(2)}, u32[]{:S(2)}) collective-permute-start(f32[4,8,224]{1,0,2:T(4,128)S(1)} %collective-permute-done.1), channel_id=1, source_target_pairs={{0,1},{1,2},{2,3},{3,4},{4,5},{5,6},{6,7},{7,8},{8,9},{9,10},{10,1... | collective-permute-start | bytes 86024 | tf_op jit(solution)/shard_map/ppermute | solution.py:57
  33.7 12.1 %collective-permute-start.10 = (f32[4,8,224]{1,0,2:T(4,128)S(1)}, f32[4,8,224]{1,0,2:T(4,128)S(1)}, u32[]{:S(2)}, u32[]{:S(2)}) collective-permute-start(f32[4,8,224]{1,0,2:T(4,128)S(1)} %collective-permute-done.9), channel_id=1, source_target_pairs={{0,15},{1,0},{2,1},{3,2},{4,3},{5,4},{6,5},{7,6},{8,7},{9,8},{10,9... | collective-permute-start | bytes 86024 | tf_op jit(solution)/shard_map/ppermute | solution.py:59
  41.4 55.7 %copy-start = (f32[4,8,224]{1,0,2:T(4,128)}, f32[4,8,224]{1,0,2:T(4,128)S(1)}, u32[]{:S(2)}) copy-start(f32[4,8,224]{1,0,2:T(4,128)S(1)} %collective-permute-done.2) | copy-start | bytes 86020
  41.4 10.7 %collective-permute-start.3 = (f32[4,8,224]{1,0,2:T(4,128)S(1)}, f32[4,8,224]{1,0,2:T(4,128)S(1)}, u32[]{:S(2)}, u32[]{:S(2)}) collective-permute-start(f32[4,8,224]{1,0,2:T(4,128)S(1)} %collective-permute-done.2), channel_id=1, source_target_pairs={{0,1},{1,2},{2,3},{3,4},{4,5},{5,6},{6,7},{7,8},{8,9},{9,10},{10,1... | collective-permute-start | bytes 86024 | tf_op jit(solution)/shard_map/ppermute | solution.py:57
  45.8 51.3 %copy-start.1 = (f32[4,8,224]{1,0,2:T(4,128)}, f32[4,8,224]{1,0,2:T(4,128)S(1)}, u32[]{:S(2)}) copy-start(f32[4,8,224]{1,0,2:T(4,128)S(1)} %collective-permute-done.10) | copy-start | bytes 86020
  45.8 12.8 %collective-permute-start.11 = (f32[4,8,224]{1,0,2:T(4,128)S(1)}, f32[4,8,224]{1,0,2:T(4,128)S(1)}, u32[]{:S(2)}, u32[]{:S(2)}) collective-permute-start(f32[4,8,224]{1,0,2:T(4,128)S(1)} %collective-permute-done.10), channel_id=1, source_target_pairs={{0,15},{1,0},{2,1},{3,2},{4,3},{5,4},{6,5},{7,6},{8,7},{9,8},{10,9... | collective-permute-start | bytes 86024 | tf_op jit(solution)/shard_map/ppermute | solution.py:59
  52.0 6.6 %copy-start.2 = (f32[4,8,224]{1,0,2:T(4,128)}, f32[4,8,224]{1,0,2:T(4,128)S(1)}, u32[]{:S(2)}) copy-start(f32[4,8,224]{1,0,2:T(4,128)S(1)} %collective-permute-done.3) | copy-start | bytes 86020
  52.0 10.6 %collective-permute-start.4 = (f32[4,8,224]{1,0,2:T(4,128)S(1)}, f32[4,8,224]{1,0,2:T(4,128)S(1)}, u32[]{:S(2)}, u32[]{:S(2)}) collective-permute-start(f32[4,8,224]{1,0,2:T(4,128)S(1)} %collective-permute-done.3), channel_id=1, source_target_pairs={{0,1},{1,2},{2,3},{3,4},{4,5},{5,6},{6,7},{7,8},{8,9},{9,10},{10,1... | collective-permute-start | bytes 86024 | tf_op jit(solution)/shard_map/ppermute | solution.py:57
  58.6 4.0 %copy-start.3 = (f32[4,8,224]{1,0,2:T(4,128)}, f32[4,8,224]{1,0,2:T(4,128)S(1)}, u32[]{:S(2)}) copy-start(f32[4,8,224]{1,0,2:T(4,128)S(1)} %collective-permute-done.11) | copy-start | bytes 86020
  58.6 12.8 %collective-permute-start.12 = (f32[4,8,224]{1,0,2:T(4,128)S(1)}, f32[4,8,224]{1,0,2:T(4,128)S(1)}, u32[]{:S(2)}, u32[]{:S(2)}) collective-permute-start(f32[4,8,224]{1,0,2:T(4,128)S(1)} %collective-permute-done.11), channel_id=1, source_target_pairs={{0,15},{1,0},{2,1},{3,2},{4,3},{5,4},{6,5},{7,6},{8,7},{9,8},{10,9... | collective-permute-start | bytes 86024 | tf_op jit(solution)/shard_map/ppermute | solution.py:59
  62.6 8.8 %copy-start.4 = (f32[4,8,224]{1,0,2:T(4,128)}, f32[4,8,224]{1,0,2:T(4,128)S(1)}, u32[]{:S(2)}) copy-start(f32[4,8,224]{1,0,2:T(4,128)S(1)} %collective-permute-done.4) | copy-start | bytes 86020
  62.6 11.0 %collective-permute-start.5 = (f32[4,8,224]{1,0,2:T(4,128)S(1)}, f32[4,8,224]{1,0,2:T(4,128)S(1)}, u32[]{:S(2)}, u32[]{:S(2)}) collective-permute-start(f32[4,8,224]{1,0,2:T(4,128)S(1)} %collective-permute-done.4), channel_id=1, source_target_pairs={{0,1},{1,2},{2,3},{3,4},{4,5},{5,6},{6,7},{7,8},{8,9},{9,10},{10,1... | collective-permute-start | bytes 86024 | tf_op jit(solution)/shard_map/ppermute | solution.py:57
  71.4 12.8 %collective-permute-start.13 = (f32[4,8,224]{1,0,2:T(4,128)S(1)}, f32[4,8,224]{1,0,2:T(4,128)}, u32[]{:S(2)}, u32[]{:S(2)}) collective-permute-start(f32[4,8,224]{1,0,2:T(4,128)S(1)} %collective-permute-done.12), channel_id=1, source_target_pairs={{0,15},{1,0},{2,1},{3,2},{4,3},{5,4},{6,5},{7,6},{8,7},{9,8},{10,9... | collective-permute-start | bytes 86024 | tf_op jit(solution)/shard_map/ppermute | solution.py:59
  73.6 10.6 %copy-start.6 = (f32[4,8,224]{1,0,2:T(4,128)}, f32[4,8,224]{1,0,2:T(4,128)S(1)}, u32[]{:S(2)}) copy-start(f32[4,8,224]{1,0,2:T(4,128)S(1)} %collective-permute-done.5) | copy-start | bytes 86020
  73.6 12.9 %collective-permute-start.6 = (f32[4,8,224]{1,0,2:T(4,128)S(1)}, f32[4,8,224]{1,0,2:T(4,128)}, u32[]{:S(2)}, u32[]{:S(2)}) collective-permute-start(f32[4,8,224]{1,0,2:T(4,128)S(1)} %collective-permute-done.5), channel_id=1, source_target_pairs={{0,1},{1,2},{2,3},{3,4},{4,5},{5,6},{6,7},{7,8},{8,9},{9,10},{10,1... | collective-permute-start | bytes 86024 | tf_op jit(solution)/shard_map/ppermute | solution.py:57
  84.3 12.8 %collective-permute-start.14 = (f32[4,8,224]{1,0,2:T(4,128)}, f32[4,8,224]{1,0,2:T(4,128)}, u32[]{:S(2)}, u32[]{:S(2)}) collective-permute-start(f32[4,8,224]{1,0,2:T(4,128)} %collective-permute-done.13), channel_id=1, source_target_pairs={{0,15},{1,0},{2,1},{3,2},{4,3},{5,4},{6,5},{7,6},{8,7},{9,8},{10,9... | collective-permute-start | bytes 86024 | tf_op jit(solution)/shard_map/ppermute | solution.py:59
  86.6 13.0 %collective-permute-start.7 = (f32[4,8,224]{1,0,2:T(4,128)}, f32[4,8,224]{1,0,2:T(4,128)}, u32[]{:S(2)}, u32[]{:S(2)}) collective-permute-start(f32[4,8,224]{1,0,2:T(4,128)} %collective-permute-done.6), channel_id=1, source_target_pairs={{0,1},{1,2},{2,3},{3,4},{4,5},{5,6},{6,7},{7,8},{8,9},{9,10},{10,1... | collective-permute-start | bytes 86024 | tf_op jit(solution)/shard_map/ppermute | solution.py:57
  135.5 6.9 %copy-start.7 = (f32[224]{0:T(256)S(1)}, f32[224]{0:T(256)}, u32[]{:S(2)}) copy-start(f32[224]{0:T(256)} %param.10) | copy-start | bytes 2692
  135.5 6.9 %copy-start.8 = (f32[128]{0:T(128)S(1)}, f32[128]{0:T(128)}, u32[]{:S(2)}) copy-start(f32[128]{0:T(128)} %param.9) | copy-start | bytes 1540
  (1 other events, 2.2 us)
Sparse Core Ops, SparseCore 0:
  142.5 96.3 all-reduce.1
